TPU v7x, 32 devices: a whole 2x2x4 slice. The times are simulated.
32 devices in a mesh: grp: 2 (over y), rx: 4 (over z), tw: 2 (over x), fq: 2 (over core).
Axes of the slice: x: 2, y: 2, z: 4, core: 2. Of those that a mesh axis runs over, the one named last changes fastest.
Arguments:
- traces: bfloat16 [8, 256, 15360], P('tw', ('grp', 'rx')), parts along dimension 1, may hold values from -48 to 48
- src_index: int32 [8, 64], P('grp'), parts along dimension 0, may hold values from 0 to 127
- valid: int32 [8, 256], P(None, 'grp'), parts along dimension 1, may hold values from 0 to 1, as said below
Outputs:
- correlations: bfloat16 [256, 256, 512], P(('tw', 'fq'), ('grp', 'rx')), parts along dimension 1
There are 2 independent parts, one for each index of `grp`. A program takes and returns all parts, laid end to end along the dimension named above; each array names one. Nothing has to cross between parts.
Inputs may be any that keep to these rules, and one draw needn't show every extreme that they name: `valid`: some channels may be 0 in every window, and some windows 0 on every channel. `src_index`: A channel may be named by several sources.
All inputs are finite; a program needn't handle non-finite values.
Results may differ from a plain program's by a relative error of at most 0.0062.
Values may be sent and summed in bfloat16 or wider, within the bound.
No kernel may reach another device: no remote copies, remote signals or barrier semaphores. Data moves between devices by JAX's collectives and lax.ppermute only.
A program may use at most 128 MiB of HBM per device.

v0:
```python
import math
import jax
import jax.numpy as jnp
from jax import lax
from jax.sharding import PartitionSpec as P

NT = 15360
BAND = 512
F0 = 60
HW = 32
LAGS = 512
two_pi = 2.0 * math.pi
eps_power = 1e-05


def padded_2(block, sides, width):
    for axis, dim in sides:
        count = lax.axis_size(axis)
        forward = [(i, i + 1) for i in range(count - 1)]
        backward = [(target, source) for source, target in forward]
        low = lax.ppermute(
            lax.slice_in_dim(block, block.shape[dim] - width, None, axis=dim), axis, forward
        )
        high = lax.ppermute(lax.slice_in_dim(block, 0, width, axis=dim), axis, backward)
        block = jnp.concatenate([low, block, high], axis=dim)
    return block


def forward_block(row_count, bin_ids, period):
    sample_ids = lax.broadcasted_iota(jnp.int32, (row_count, 1, 1), 0)
    phase_index = sample_ids * bin_ids[None, :, :] % period
    angle_rad = phase_index.astype(jnp.float32) * (two_pi / period)
    coef_block = jnp.stack([jnp.cos(angle_rad), -jnp.sin(angle_rad)], axis=2)
    return coef_block.reshape(row_count, -1).astype(jnp.bfloat16)


def inverse_rows(bin_ids, lag_count, period):
    lag_shift = lax.broadcasted_iota(jnp.int32, (1, lag_count), 1) - lag_count // 2
    phase_index = bin_ids[..., None] * lag_shift % period
    angle_rad = phase_index.astype(jnp.float32) * (two_pi / period)
    return jnp.concatenate([jnp.cos(angle_rad), -jnp.sin(angle_rad)], axis=-2).astype(jnp.bfloat16)


def shards(traces, src_index, valid):
    win_count, chan_count, samples = traces.shape
    tw_count = lax.axis_size("tw")
    fq_count = lax.axis_size("fq")
    tw_pos = lax.axis_index("tw")
    fq_pos = lax.axis_index("fq")
    rx_pos = lax.axis_index("rx")
    band_share = BAND // fq_count
    narrow = band_share // tw_count
    block_len = 1024
    trace_rows = traces.reshape(win_count * chan_count, samples)
    local_bins = (
        F0
        + fq_pos * band_share
        + lax.broadcasted_iota(jnp.int32, (tw_count, narrow), 0) * narrow
        + lax.broadcasted_iota(jnp.int32, (tw_count, narrow), 1)
    )
    base_table = forward_block(block_len, local_bins, samples)

    def accumulate(turn_index, running):
        offset = turn_index * block_len
        trace_piece = lax.dynamic_slice_in_dim(trace_rows, offset, block_len, 1)
        partial_value = jnp.dot(trace_piece, base_table, preferred_element_type=jnp.float32)
        partial_value = partial_value.reshape(-1, tw_count, 2, narrow)
        part_real = partial_value[:, :, 0]
        part_imag = partial_value[:, :, 1]
        phase_index = offset * local_bins % samples
        angle_rad = phase_index.astype(jnp.float32) * (two_pi / samples)
        turn_real = jnp.cos(angle_rad)[None]
        turn_imag = -jnp.sin(angle_rad)[None]
        new_real = part_real * turn_real - part_imag * turn_imag
        new_imag = part_real * turn_imag + part_imag * turn_real
        return running + jnp.stack([new_real, new_imag], axis=2)

    spec_parts = lax.fori_loop(
        0,
        samples // block_len,
        accumulate,
        jnp.zeros((win_count * chan_count, tw_count, 2, narrow), jnp.float32),
    )
    bin_power = (
        spec_parts[:, :, 0] * spec_parts[:, :, 0] + spec_parts[:, :, 1] * spec_parts[:, :, 1]
    )
    bin_power = bin_power.reshape(-1, band_share)
    padded = padded_2(bin_power, (("fq", 1),), HW)
    row_ids = lax.broadcasted_iota(jnp.int32, (band_share + 2 * HW, band_share), 0)
    col_ids = lax.broadcasted_iota(jnp.int32, (band_share + 2 * HW, band_share), 1)
    box_matrix = ((row_ids - col_ids >= 0) & (row_ids - col_ids <= 2 * HW)).astype(jnp.float32)
    smooth = jnp.dot(
        padded, box_matrix, precision=lax.Precision.HIGHEST, preferred_element_type=jnp.float32
    ) / (2 * HW + 1)
    white_gain = lax.rsqrt(smooth + eps_power).reshape(-1, tw_count, 1, narrow)
    whitened = (
        (spec_parts * white_gain)
        .astype(jnp.bfloat16)
        .reshape(win_count, chan_count, tw_count, 2 * narrow)
    )
    valid_float = valid.astype(jnp.float32)
    source_ids = src_index.reshape(-1)
    src_total = source_ids.shape[0]
    channels_all = valid.shape[1]
    pick_all = (
        lax.broadcasted_iota(jnp.int32, (channels_all, src_total), 0) == source_ids[None, :]
    ).astype(jnp.float32)
    source_valid = jnp.dot(
        valid_float, pick_all, precision=lax.Precision.HIGHEST, preferred_element_type=jnp.float32
    )
    receiver_valid = lax.dynamic_slice_in_dim(valid_float, rx_pos * chan_count, chan_count, 1)
    pair_count = jnp.dot(
        source_valid.T,
        receiver_valid,
        precision=lax.Precision.HIGHEST,
        preferred_element_type=jnp.float32,
    )
    pair_floor = jnp.maximum(pair_count, 1.0)[:, :, None]
    pick_local = (
        source_ids[:, None]
        == rx_pos * chan_count + lax.broadcasted_iota(jnp.int32, (1, chan_count), 1)
    ).astype(jnp.bfloat16)
    inv_scale = 1.0 / math.sqrt(BAND)
    own_block = tw_pos * fq_count + fq_pos
    src_local = src_total // (tw_count * fq_count)
    local_terms = jnp.einsum(
        "sc,wcx->swx",
        pick_local,
        whitened.reshape(win_count, chan_count, tw_count * 2 * narrow),
        preferred_element_type=jnp.float32,
    )
    sources = lax.psum(local_terms.astype(jnp.bfloat16), "rx")
    own_sources = lax.all_to_all(
        sources[None], ("tw", "fq"), split_axis=1, concat_axis=0, tiled=True
    )
    all_windows = lax.all_gather(whitened[None], ("tw", "fq"), axis=0, tiled=True)
    src_valid_own = lax.dynamic_slice_in_dim(source_valid, own_block * src_local, src_local, 1)
    src_valid_own = jnp.transpose(src_valid_own.reshape(tw_count, win_count, src_local), (0, 2, 1))
    own_sources = own_sources.reshape(
        tw_count, fq_count, src_local, win_count, tw_count, 2, narrow
    ) * src_valid_own.reshape(tw_count, 1, src_local, win_count, 1, 1, 1).astype(jnp.bfloat16)
    all_windows = all_windows.reshape(
        tw_count, fq_count, win_count, chan_count, tw_count, 2, narrow
    ) * receiver_valid.reshape(tw_count, 1, win_count, chan_count, 1, 1, 1).astype(jnp.bfloat16)
    src_real = own_sources[..., 0, :]
    src_imag = own_sources[..., 1, :]
    rec_real = all_windows[..., 0, :]
    rec_imag = all_windows[..., 1, :]
    pattern = "tfswbx,tfwcbx->scfbx"
    cross_real = jnp.einsum(
        pattern, src_real, rec_real, preferred_element_type=jnp.float32
    ) + jnp.einsum(pattern, src_imag, rec_imag, preferred_element_type=jnp.float32)
    cross_imag = jnp.einsum(
        pattern, src_real, rec_imag, preferred_element_type=jnp.float32
    ) - jnp.einsum(pattern, src_imag, rec_real, preferred_element_type=jnp.float32)
    floor_own = lax.dynamic_slice_in_dim(pair_floor, own_block * src_local, src_local, 0)
    stacked = jnp.concatenate(
        [
            cross_real.reshape(src_local, chan_count, BAND),
            cross_imag.reshape(src_local, chan_count, BAND),
        ],
        axis=2,
    )
    stacked = (stacked / floor_own).astype(jnp.bfloat16)
    inv_table = inverse_rows(F0 + lax.broadcasted_iota(jnp.int32, (BAND,), 0), LAGS, NT)
    summed = jnp.dot(
        stacked.reshape(src_local * chan_count, 2 * BAND),
        inv_table,
        preferred_element_type=jnp.float32,
    ).reshape(src_local, chan_count, LAGS)
    return (summed * inv_scale).astype(jnp.bfloat16)


def solution(mesh):
    return jax.shard_map(
        shards,
        mesh=mesh,
        in_specs=(P("tw", ("grp", "rx"), None), P("grp", None), P(None, "grp")),
        out_specs=P(("tw", "fq"), ("grp", "rx"), None),
        check_vma=False,
    )
```

profile of v0, /device:TPU:0, one launch (start us, length us, event | category | flops | bytes accessed | tf_op | source)
XLA Modules:
  0.0 195.9 jit_solution(17614216192900421187)
XLA Ops:
  6.6 4.6 %cosine_convert_fusion.1 = (bf16[1024,2,1,128]{3,0,2,1:T(8,128)(2,1)S(1)}, bf16[1024,2,1,128]{3,0,2,1:T(8,128)(2,1)S(1)}) fusion(s32[2,128]{1,0:T(2,128)S(1)} %iota_add_fusion.2), kind=kLoop, calls=%fused_computation.47 | loop fusion | flops 3145728 | bytes 1049600 | tf_op jit(solution)/shard_map/convert.2
  11.3 0.5 copy.35
  11.8 0.5 copy.36
  12.4 34.7 %while.16 = (s32[]{:T(128)}, f32[128,2,2,128]{3,2,1,0:T(2,128)S(1)}, bf16[128,15360]{1,0:T(8,128)(2,1)}, bf16[1024,512]{1,0:T(8,128)(2,1)S(1)}, s32[2]{0:T(128)S...) while((s32[]{:T(128)}, f32[128,2,2,128]{3,2,1,0:T(2,128)S(1)}, ...), condition=%wide.region_1.2_spmd.clone, body=%wide.region_0.1_spmd.clone.sunk | while | flops 134613760 | bytes 3412133 | solution.py:78
  12.4 1.3 fusion.68
  14.0 0.3 multiply_subtract_fusion.2
  14.3 0.4 maximum_add_fusion.2
  14.7 1.3 fusion.68
  16.3 0.3 multiply_subtract_fusion.2
  16.6 0.4 maximum_add_fusion.2
  17.1 1.3 fusion.68
  18.6 0.3 multiply_subtract_fusion.2
  18.9 0.4 maximum_add_fusion.2
  19.4 1.3 fusion.68
  20.9 0.3 multiply_subtract_fusion.2
  21.2 0.4 maximum_add_fusion.2
  21.7 1.3 fusion.68
  23.3 0.3 multiply_subtract_fusion.2
  23.5 0.4 maximum_add_fusion.2
  24.0 1.3 fusion.68
  25.6 0.3 multiply_subtract_fusion.2
  25.9 0.4 maximum_add_fusion.2
  26.3 1.3 fusion.68
  28.2 0.4 maximum_add_fusion.2
  28.6 1.3 fusion.68
  30.5 0.4 maximum_add_fusion.2
  31.0 1.3 fusion.68
  32.8 0.4 maximum_add_fusion.2
  33.3 1.3 fusion.68
  35.1 0.4 maximum_add_fusion.2
  35.6 1.3 fusion.68
  37.4 0.4 maximum_add_fusion.2
  37.9 1.3 fusion.68
  39.8 0.4 maximum_add_fusion.2
  40.2 1.3 fusion.68
  42.1 0.4 maximum_add_fusion.2
  42.5 1.3 fusion.68
  44.4 0.4 maximum_add_fusion.2
  44.8 1.3 fusion.68
  46.7 0.4 maximum_add_fusion.2
  47.1 0.5 add_reduce_fusion
  47.8 2.4 %collective-permute-start = (f32[128,32]{1,0:T(8,128)S(1)}, f32[128,32]{1,0:T(8,128)S(1)}, u32[]{:S(2)}, u32[]{:S(2)}) collective-permute-start(f32[128,32]{1,0:T(8,128)S(1)} %get-tuple-element.179), channel_id=1, source_target_pairs={{0,1},{2,3},{4,5},{6,7},{8,9},{10,11},{12,13},{14,15},{16,17},{18,... | collective-permute-start | bytes 49160 | tf_op jit(solution)/shard_map/ppermute | solution.py:21
  50.2 1.3 collective-permute-start.1
  51.6 1.7 collective-permute-done.1
  53.3 0.3 fusion.16
  54.0 1.5 fusion.14
  55.7 0.3 fusion.49
  56.1 53.5 %all-reduce.2.cloned.1.call-done = bf16[1,256,4,512]{3,1,2,0:T(8,128)(2,1)} async-done(((bf16[1,256,4,512]{3,1,2,0:T(8,128)(2,1)}), bf16[1,256,4,512]{3,1,2,0:T(8,128)(2,1)}) %all-reduce.2.cloned.1.call-update) | async-done | bytes 1048592 | tf_op jit(solution)/shard_map/psum | solution.py:132
  109.7 3.0 %copy.40 = bf16[1,256,4,512]{3,2,0,1:T(4,128)(2,1)} copy(bf16[1,256,4,512]{3,1,2,0:T(8,128)(2,1)} %all-reduce.2.cloned.1.call-done) | data formatting | bytes 2097152 | tf_op jit(solution)/shard_map/psum | solution.py:132
  112.7 4.3 %all-to-all-start = ((bf16[1,256,4,512]{3,2,0,1:T(4,128)(2,1)}), bf16[1,256,4,512]{3,2,0,1:T(4,128)(2,1)}, u32[]{:S(2)}, u32[]{:S(2)}) async-start(bf16[1,256,4,512]{3,2,0,1:T(4,128)(2,1)} %copy.40), calls=%async_computation | async-start | bytes 2097152 | tf_op jit(solution)/shard_map/all_to_all | solution.py:133
  117.1 5.7 %cosine_convert_fusion = (bf16[512,512]{1,0:T(8,128)(2,1)}, bf16[512,512]{1,0:T(8,128)(2,1)}) fusion(s32[512]{0:T(512)S(1)} %get-tuple-element.185, s32[512]{0:T(512)S(1)} %get-tuple-element.186), kind=kLoop, calls=%fused_computation.40 | loop fusion | flops 3145728 | bytes 1052672 | tf_op jit(solution)/shard_map/convert
  123.0 12.0 %all_gather.3 = bf16[4,4,32,2,256]{4,2,3,1,0:T(8,128)(2,1)S(1)} all-gather(bf16[1,4,32,2,256]{4,2,3,1,0:T(8,128)(2,1)S(1)} %copy.38), channel_id=1, replica_groups=mesh['grp'=2,'rx'=4,'tw'=2,'fq'=2] {'tw','fq'}, dimensions={0}, use_global_device_ids=true | all-gather | bytes 655360 | tf_op jit(solution)/shard_map/all_gather | solution.py:136
  135.1 2.5 %copy.39 = bf16[2,2,4,32,2,2,128]{3,2,0,6,4,1,5:T(4,128)(2,1)} copy(bf16[2,2,4,32,2,2,128]{6,5,3,4,2,1,0:T(2,128)(2,1)S(1)} %reshape.161) | data formatting | bytes 1048576 | tf_op jit(solution)/shard_map/reshape | solution.py:142
  137.7 1.7 broadcast_multiply_fusion.1
  139.4 1.5 reshape.171
  140.9 4.3 %copy.42 = bf16[2,2,64,4,2,2,128]{2,3,0,6,4,1,5:T(4,128)(2,1)} copy(bf16[2,2,64,4,2,2,128]{6,5,4,3,2,1,0:T(2,128)(2,1)S(1)} %reshape.171) | data formatting | bytes 2097152 | tf_op jit(solution)/shard_map/reshape | solution.py:139
  145.1 1.7 broadcast_multiply_fusion
  146.9 1.8 fusion.29
  148.7 4.2 %fusion.30 = f32[2,2,128,32,64,1]{4,3,5,2,1,0:T(8,128)} fusion(bf16[2,2,64,4,2,2,128]{2,3,0,6,4,1,5:T(4,128)(2,1)S(1)} %bitcast.78, bf16[2,2,4,32,2,2,128]{3,2,0,6,4,1,5:T(4,128)(2,1)S(1)} %bitcast.74), kind=kOutput, calls=%fused_computation.54 | convolution fusion | flops 16777216 | bytes 6291456 | tf_op jit(solution)/shard_map/tfswbx,tfwcbx->scfbx/dot_general | solution.py:153
  152.9 4.3 %bitcast_add_fusion = f32[2,2,128,32,64]{4,3,2,1,0:T(8,128)} fusion(f32[2,2,128,32,64,1]{4,3,5,2,1,0:T(8,128)S(1)} %fusion.29, bf16[2,2,4,32,2,2,128]{3,2,0,6,4,1,5:T(4,128)(2,1)S(1)} %bitcast.75, bf16[2,2,64,4,2,2,128]{2,3,0,6,4,1,5:T(4,128)(2,1)S(1)} %bitcast.79), kind=kOutput, calls=%fused_computation.17 | convolution fusion | flops 17825792 | bytes 14680064 | tf_op jit(solution)/shard_map/tfswbx,tfwcbx->scfbx/dot_general | solution.py:152
  157.2 7.7 %copy.43 = f32[64,32,512]{2,1,0:T(8,128)} copy(f32[64,32,512]{0,1,2:T(8,128)} %bitcast.72) | data formatting | bytes 8388608 | tf_op jit(solution)/shard_map/concatenate | solution.py:157
  165.0 9.1 %bitcast_subtract_fusion = f32[2,2,128,32,64]{4,3,2,1,0:T(8,128)} fusion(f32[2,2,128,32,64,1]{4,3,5,2,1,0:T(8,128)} %fusion.30, bf16[2,2,4,32,2,2,128]{3,2,0,6,4,1,5:T(4,128)(2,1)S(1)} %bitcast.76, bf16[2,2,64,4,2,2,128]{2,3,0,6,4,1,5:T(4,128)(2,1)} %bitcast.80), kind=kOutput, calls=%fused_computation.16 | convolution fusion | flops 17825792 | bytes 14680064 | tf_op jit(solution)/shard_map/tfswbx,tfwcbx->scfbx/dot_general | solution.py:155
  174.0 7.8 %copy.44 = f32[64,32,512]{2,1,0:T(8,128)} copy(f32[64,32,512]{0,1,2:T(8,128)} %bitcast.71) | data formatting | bytes 8388608 | tf_op jit(solution)/shard_map/concatenate | solution.py:157
  181.8 7.2 %multiply_convert_fusion = bf16[64,32,512]{2,1,0:T(8,128)(2,1)} fusion(f32[64,32,512]{2,1,0:T(8,128)} %copy.44, f32[64,32,512]{2,1,0:T(8,128)} %copy.43, f32[64,32]{1,0:T(8,128)S(1)} %copy.45, bf16[512,512]{1,0:T(8,128)(2,1)S(1)} %copy-done.2, bf16[512,512]{1,0:T(8,128)(2,1)S(1)} %copy-done.1), kind=kOutput, calls=%fused_computation.18 | convolution fusion | flops 2157969408 | bytes 11542528 | tf_op jit(solution)/shard_map/dot_general | solution.py:166
  (74 shorter events, 8.2 us)
Async XLA Ops:
  6.5 103.1 %all-reduce.2.cloned.1.call-start = ((), (), s32[]{:S(2)}) async-start(), calls=%async_computation.1 | async-start | bytes 2097152 | tf_op jit(solution)/shard_map/psum | solution.py:132
  12.4 39.1 %copy-start.4 = (s32[4,64]{1,0:T(4,128)S(1)}, s32[4,64]{1,0:T(4,128)}, u32[]{:S(2)}) copy-start(s32[4,64]{1,0:T(4,128)} %param.6) | copy-start | bytes 3076
  47.7 7.8 %copy-start.3 = (s32[8,128]{1,0:T(8,128)S(1)}, s32[8,128]{1,0:T(8,128)}, u32[]{:S(2)}) copy-start(s32[8,128]{1,0:T(8,128)} %param.7) | copy-start | bytes 12292
  47.8 3.8 %collective-permute-start = (f32[128,32]{1,0:T(8,128)S(1)}, f32[128,32]{1,0:T(8,128)S(1)}, u32[]{:S(2)}, u32[]{:S(2)}) collective-permute-start(f32[128,32]{1,0:T(8,128)S(1)} %get-tuple-element.179), channel_id=1, source_target_pairs={{0,1},{2,3},{4,5},{6,7},{8,9},{10,11},{12,13},{14,15},{16,17},{18,... | collective-permute-start | bytes 49160 | tf_op jit(solution)/shard_map/ppermute | solution.py:21
  50.2 3.1 %collective-permute-start.1 = (f32[128,32]{1,0:T(8,128)S(1)}, f32[128,32]{1,0:T(8,128)S(1)}, u32[]{:S(2)}, u32[]{:S(2)}) collective-permute-start(f32[128,32]{1,0:T(8,128)S(1)} %get-tuple-element.180), channel_id=1, source_target_pairs={{1,0},{3,2},{5,4},{7,6},{9,8},{11,10},{13,12},{15,14},{17,16},{19,... | collective-permute-start | bytes 49160 | tf_op jit(solution)/shard_map/ppermute | solution.py:24
  112.7 26.7 %all-to-all-start = ((bf16[1,256,4,512]{3,2,0,1:T(4,128)(2,1)}), bf16[1,256,4,512]{3,2,0,1:T(4,128)(2,1)}, u32[]{:S(2)}, u32[]{:S(2)}) async-start(bf16[1,256,4,512]{3,2,0,1:T(4,128)(2,1)} %copy.40), calls=%async_computation | async-start | bytes 2097152 | tf_op jit(solution)/shard_map/all_to_all | solution.py:133
  146.9 6.0 %copy-start = (bf16[1,2,64,8,2,2,128]{2,3,0,6,4,1,5:T(8,128)(2,1)}, bf16[1,2,64,8,2,2,128]{2,3,0,6,4,1,5:T(8,128)(2,1)S(1)}, u32[]{:S(2)}) copy-start(bf16[1,2,64,8,2,2,128]{2,3,0,6,4,1,5:T(8,128)(2,1)S(1)} %broadcast_multiply_fusion) | copy-start | bytes 3145732
  174.0 7.8 %copy-start.1 = (bf16[512,512]{1,0:T(8,128)(2,1)S(1)}, bf16[512,512]{1,0:T(8,128)(2,1)}, u32[]{:S(2)}) copy-start(bf16[512,512]{1,0:T(8,128)(2,1)} %get-tuple-element.181) | copy-start | bytes 1572868
  174.0 7.8 %copy-start.2 = (bf16[512,512]{1,0:T(8,128)(2,1)S(1)}, bf16[512,512]{1,0:T(8,128)(2,1)}, u32[]{:S(2)}) copy-start(bf16[512,512]{1,0:T(8,128)(2,1)} %get-tuple-element.182) | copy-start | bytes 1572868
Sparse Core Ops, SparseCore 0:
  55.6 54.0 all-reduce.1
where the time goes:
time: 197 us; the launch traced here: 196 us
  waiting for transfers between devices  55.3 us (28%)
  matrix products  47.8 us (24%)
  local copies, waits for them, and re-layouts  31.2 us (16%)
  other arithmetic  27.4 us (14%)
  between operations  13.6 us (7%)
  blocking collectives  12 us (6%)
  starting transfers between devices  7.95 us (4%)
    psum x1, waiting for transfers between devices, shards(): sources = lax.psum(local_terms.astype(jnp.bfloat16), 'rx')  53.5 us
    dot_general x15, matrix products, accumulate(): jnp.dot(trace_piece, base_table, preferred_element_type=jnp.float32)  18.9 us
    concatenate x2, local copies, waits for them, and re-layouts, shards(): jnp.concatenate([cross_real.reshape(src_local, chan_count, BAND), cross_i...  15.5 us
    all_gather x1, blocking collectives, shards(): lax.all_gather(whitened[None], ('tw', 'fq'), axis=0, tiled=True)  12 us
    another operation x2, other arithmetic  10.3 us
    dot_general x1, matrix products, shards(): jnp.einsum(pattern, src_imag, rec_real, preferred_element_type=jnp.float32)  9.08 us
    dot_general x1, matrix products, shards(): jnp.dot(stacked.reshape(src_local * chan_count, 2 * BAND), inv_table, pre...  7.22 us
    add x15, other arithmetic, accumulate(): return running + jnp.stack([new_real, new_imag], axis=2)  6.72 us
  transfers between devices with their start and end apart: 4, of which 2 were waited for; matrix products, arithmetic and copies ran while one was open for 6% of the time, Pallas kernels for 0%

commit v1 on v0

--- a/solution.py
+++ b/solution.py
@@ -129,7 +129,8 @@
         whitened.reshape(win_count, chan_count, tw_count * 2 * narrow),
         preferred_element_type=jnp.float32,
     )
-    sources = lax.psum(local_terms.astype(jnp.bfloat16), "rx")
+    buf = local_terms.astype(jnp.bfloat16)
+    sources = jnp.sum(lax.all_gather(buf, axis_name="rx"), axis=0)
     own_sources = lax.all_to_all(
         sources[None], ("tw", "fq"), split_axis=1, concat_axis=0, tiled=True
     )

time: 197 us -> 227 us (1.15)
  waiting for transfers between devices: 55.3 us -> 84.1 us
  other arithmetic: 27.4 us -> 30.4 us
    all_gather x0 -> x1, waiting for transfers between devices: none -> 82.3 us  [shards(): sources = jnp.sum(lax.all_gather(buf, axis_name='rx'), axis=0)]
    psum x1 -> x0, waiting for transfers between devices: 53.5 us -> none  [shards(): sources = lax.psum(local_terms.astype(jnp.bfloat16), 'rx')]
    reduce_sum x0 -> x1, other arithmetic: none -> 3.02 us  [shards(): sources = jnp.sum(lax.all_gather(buf, axis_name='rx'), axis=0)]
    psum x1 -> x0, local copies, waits for them, and re-layouts: 3.01 us -> none  [shards(): sources = lax.psum(local_terms.astype(jnp.bfloat16), 'rx')]
  transfers between devices with their start and end apart: 4 -> 4, of which waited for: 2 -> 2; matrix products, arithmetic and copies ran while one was open for 6% -> 5% of each run, Pallas kernels for 0% -> 0%
where the time goes in v1:
time: 227 us; the launch traced here: 226 us
  waiting for transfers between devices  84.1 us (37%)
  matrix products  47.8 us (21%)
  other arithmetic  30.4 us (13%)
  local copies, waits for them, and re-layouts  30 us (13%)
  between operations  13.6 us (6%)
  blocking collectives  12 us (5%)
  starting transfers between devices  7.93 us (3%)
    all_gather x1, waiting for transfers between devices, shards(): sources = jnp.sum(lax.all_gather(buf, axis_name='rx'), axis=0)  82.3 us
    dot_general x15, matrix products, accumulate(): jnp.dot(trace_piece, base_table, preferred_element_type=jnp.float32)  18.9 us
    concatenate x2, local copies, waits for them, and re-layouts, shards(): jnp.concatenate([cross_real.reshape(src_local, chan_count, BAND), cross_i...  15.5 us
    all_gather x1, blocking collectives, shards(): lax.all_gather(whitened[None], ('tw', 'fq'), axis=0, tiled=True)  12 us
    another operation x2, other arithmetic  10.3 us
    dot_general x1, matrix products, shards(): jnp.einsum(pattern, src_imag, rec_real, preferred_element_type=jnp.float32)  9.08 us
    dot_general x1, matrix products, shards(): jnp.dot(stacked.reshape(src_local * chan_count, 2 * BAND), inv_table, pre...  7.22 us
    add x15, other arithmetic, accumulate(): return running + jnp.stack([new_real, new_imag], axis=2)  6.72 us
  transfers between devices with their start and end apart: 4, of which 2 were waited for; matrix products, arithmetic and copies ran while one was open for 5% of the time, Pallas kernels for 0%

profile of v1, /device:TPU:0, one launch (start us, length us, event | category | flops | bytes accessed | tf_op | source)
XLA Modules:
  0.0 226.5 jit_solution(16384148249282480802)
XLA Ops:
  6.6 4.6 %cosine_convert_fusion.1 = (bf16[1024,2,1,128]{3,0,2,1:T(8,128)(2,1)S(1)}, bf16[1024,2,1,128]{3,0,2,1:T(8,128)(2,1)S(1)}) fusion(s32[2,128]{1,0:T(2,128)S(1)} %iota_add_fusion.2), kind=kLoop, calls=%fused_computation.46 | loop fusion | flops 3145728 | bytes 1049600 | tf_op jit(solution)/shard_map/convert.3
  11.3 0.5 copy.43
  11.8 0.5 copy.44
  12.4 34.7 %while.16 = (s32[]{:T(128)}, f32[128,2,2,128]{3,2,1,0:T(2,128)S(1)}, bf16[128,15360]{1,0:T(8,128)(2,1)}, bf16[1024,512]{1,0:T(8,128)(2,1)S(1)}, s32[2]{0:T(128)S...) while((s32[]{:T(128)}, f32[128,2,2,128]{3,2,1,0:T(2,128)S(1)}, ...), condition=%wide.region_1.2_spmd.clone, body=%wide.region_0.1_spmd.clone.sunk | while | flops 134613760 | bytes 3412133 | solution.py:78
  12.4 1.3 fusion.67
  14.0 0.3 multiply_subtract_fusion.2
  14.3 0.4 maximum_add_fusion.2
  14.7 1.3 fusion.67
  16.3 0.3 multiply_subtract_fusion.2
  16.6 0.4 maximum_add_fusion.2
  17.1 1.3 fusion.67
  18.6 0.3 multiply_subtract_fusion.2
  18.9 0.4 maximum_add_fusion.2
  19.4 1.3 fusion.67
  20.9 0.3 multiply_subtract_fusion.2
  21.2 0.4 maximum_add_fusion.2
  21.7 1.3 fusion.67
  23.3 0.3 multiply_subtract_fusion.2
  23.5 0.4 maximum_add_fusion.2
  24.0 1.3 fusion.67
  25.9 0.4 maximum_add_fusion.2
  26.3 1.3 fusion.67
  28.2 0.4 maximum_add_fusion.2
  28.6 1.3 fusion.67
  30.5 0.4 maximum_add_fusion.2
  31.0 1.3 fusion.67
  32.8 0.4 maximum_add_fusion.2
  33.3 1.3 fusion.67
  35.1 0.4 maximum_add_fusion.2
  35.6 1.3 fusion.67
  37.4 0.4 maximum_add_fusion.2
  37.9 1.3 fusion.67
  39.8 0.4 maximum_add_fusion.2
  40.2 1.3 fusion.67
  42.1 0.4 maximum_add_fusion.2
  42.5 1.3 fusion.67
  44.4 0.4 maximum_add_fusion.2
  44.8 1.3 fusion.67
  46.7 0.4 maximum_add_fusion.2
  47.2 0.5 add_reduce_fusion
  47.8 2.4 %collective-permute-start = (f32[128,32]{1,0:T(8,128)S(1)}, f32[128,32]{1,0:T(8,128)S(1)}, u32[]{:S(2)}, u32[]{:S(2)}) collective-permute-start(f32[128,32]{1,0:T(8,128)S(1)} %get-tuple-element.179), channel_id=1, source_target_pairs={{0,1},{2,3},{4,5},{6,7},{8,9},{10,11},{12,13},{14,15},{16,17},{18,... | collective-permute-start | bytes 49160 | tf_op jit(solution)/shard_map/ppermute | solution.py:21
  50.2 1.3 collective-permute-start.1
  51.6 1.7 collective-permute-done.1
  53.3 0.3 fusion.15
  53.9 1.5 convolution_convert_fusion
  55.7 0.3 fusion.48
  56.1 82.3 %all-gather.3.cloned.1.call-done = bf16[1024,4,512]{2,0,1:T(8,128)(2,1)} async-done(((bf16[256,4,512]{2,0,1:T(8,128)(2,1)}), bf16[1024,4,512]{2,0,1:T(8,128)(2,1)}) %all-gather.3.cloned.1.call-update) | async-done | bytes 4194320 | tf_op jit(solution)/shard_map/all_gather | solution.py:133
  138.4 3.0 %reduce_sum.12 = bf16[256,4,512]{2,0,1:T(8,128)(2,1)S(1)} reduce(bf16[4,256,4,512]{3,1,0,2:T(8,128)(2,1)} %bitcast.83, bf16[]{:T(256)} %constant.125.clone.1), dimensions={0}, to_apply=%region_2.3 | reduce | flops 1572864 | bytes 5242882 | tf_op jit(solution)/shard_map/reduce_sum | solution.py:133
  141.5 1.8 copy.48
  143.3 4.2 %all-to-all-start = ((bf16[1,256,4,512]{3,2,0,1:T(4,128)(2,1)}), bf16[1,256,4,512]{3,2,0,1:T(4,128)(2,1)}, u32[]{:S(2)}, u32[]{:S(2)}) async-start(bf16[1,256,4,512]{3,2,0,1:T(4,128)(2,1)} %copy.48), calls=%async_computation | async-start | bytes 2097152 | tf_op jit(solution)/shard_map/all_to_all | solution.py:134
  147.7 5.7 %cosine_convert_fusion = (bf16[512,512]{1,0:T(8,128)(2,1)}, bf16[512,512]{1,0:T(8,128)(2,1)}) fusion(s32[512]{0:T(512)S(1)} %get-tuple-element.185, s32[512]{0:T(512)S(1)} %get-tuple-element.186), kind=kLoop, calls=%fused_computation.39 | loop fusion | flops 3145728 | bytes 1052672 | tf_op jit(solution)/shard_map/convert.1
  153.5 12.0 %all_gather.9 = bf16[4,4,32,2,256]{4,2,3,1,0:T(8,128)(2,1)S(1)} all-gather(bf16[1,4,32,2,256]{4,2,3,1,0:T(8,128)(2,1)S(1)} %copy.46), channel_id=1, replica_groups=mesh['grp'=2,'rx'=4,'tw'=2,'fq'=2] {'tw','fq'}, dimensions={0}, use_global_device_ids=true | all-gather | bytes 655360 | tf_op jit(solution)/shard_map/all_gather | solution.py:137
  165.7 2.5 %copy.47 = bf16[2,2,4,32,2,2,128]{3,2,0,6,4,1,5:T(4,128)(2,1)} copy(bf16[2,2,4,32,2,2,128]{6,5,3,4,2,1,0:T(2,128)(2,1)S(1)} %reshape.161) | data formatting | bytes 1048576 | tf_op jit(solution)/shard_map/reshape | solution.py:143
  168.3 1.7 broadcast_multiply_fusion.1
  170.0 1.5 reshape.172
  171.5 4.3 %copy.50 = bf16[2,2,64,4,2,2,128]{2,3,0,6,4,1,5:T(4,128)(2,1)} copy(bf16[2,2,64,4,2,2,128]{6,5,4,3,2,1,0:T(2,128)(2,1)S(1)} %reshape.172) | data formatting | bytes 2097152 | tf_op jit(solution)/shard_map/reshape | solution.py:140
  175.7 1.7 broadcast_multiply_fusion
  177.5 1.8 fusion.28
  179.2 4.2 %fusion.29 = f32[2,2,128,32,64,1]{4,3,5,2,1,0:T(8,128)} fusion(bf16[2,2,64,4,2,2,128]{2,3,0,6,4,1,5:T(4,128)(2,1)S(1)} %bitcast.78, bf16[2,2,4,32,2,2,128]{3,2,0,6,4,1,5:T(4,128)(2,1)S(1)} %bitcast.74), kind=kOutput, calls=%fused_computation.53 | convolution fusion | flops 16777216 | bytes 6291456 | tf_op jit(solution)/shard_map/tfswbx,tfwcbx->scfbx/dot_general | solution.py:154
  183.5 4.3 %bitcast_add_fusion = f32[2,2,128,32,64]{4,3,2,1,0:T(8,128)} fusion(f32[2,2,128,32,64,1]{4,3,5,2,1,0:T(8,128)S(1)} %fusion.28, bf16[2,2,4,32,2,2,128]{3,2,0,6,4,1,5:T(4,128)(2,1)S(1)} %bitcast.75, bf16[2,2,64,4,2,2,128]{2,3,0,6,4,1,5:T(4,128)(2,1)S(1)} %bitcast.79), kind=kOutput, calls=%fused_computation.17 | convolution fusion | flops 17825792 | bytes 14680064 | tf_op jit(solution)/shard_map/tfswbx,tfwcbx->scfbx/dot_general | solution.py:153
  187.8 7.7 %copy.51 = f32[64,32,512]{2,1,0:T(8,128)} copy(f32[64,32,512]{0,1,2:T(8,128)} %bitcast.72) | data formatting | bytes 8388608 | tf_op jit(solution)/shard_map/concatenate | solution.py:158
  195.5 9.1 %bitcast_subtract_fusion = f32[2,2,128,32,64]{4,3,2,1,0:T(8,128)} fusion(f32[2,2,128,32,64,1]{4,3,5,2,1,0:T(8,128)} %fusion.29, bf16[2,2,4,32,2,2,128]{3,2,0,6,4,1,5:T(4,128)(2,1)S(1)} %bitcast.76, bf16[2,2,64,4,2,2,128]{2,3,0,6,4,1,5:T(4,128)(2,1)} %bitcast.80), kind=kOutput, calls=%fused_computation.16 | convolution fusion | flops 17825792 | bytes 14680064 | tf_op jit(solution)/shard_map/tfswbx,tfwcbx->scfbx/dot_general | solution.py:156
  204.6 7.8 %copy.52 = f32[64,32,512]{2,1,0:T(8,128)} copy(f32[64,32,512]{0,1,2:T(8,128)} %bitcast.71) | data formatting | bytes 8388608 | tf_op jit(solution)/shard_map/concatenate | solution.py:158
  212.4 7.2 %multiply_convert_fusion = bf16[64,32,512]{2,1,0:T(8,128)(2,1)} fusion(f32[64,32,512]{2,1,0:T(8,128)} %copy.52, f32[64,32,512]{2,1,0:T(8,128)} %copy.51, f32[64,32]{1,0:T(8,128)S(1)} %copy.53, bf16[512,512]{1,0:T(8,128)(2,1)S(1)} %copy-done.2, bf16[512,512]{1,0:T(8,128)(2,1)S(1)} %copy-done.1), kind=kOutput, calls=%fused_computation.18 | convolution fusion | flops 2157969408 | bytes 11542528 | tf_op jit(solution)/shard_map/dot_general | solution.py:167
  (75 shorter events, 8.5 us)
Async XLA Ops:
  6.5 131.9 %all-gather.3.cloned.1.call-start = ((), (), s32[]{:S(2)}) async-start(), calls=%async_computation.1 | async-start | bytes 5242880 | tf_op jit(solution)/shard_map/all_gather | solution.py:133
  12.4 39.1 %copy-start.4 = (s32[4,64]{1,0:T(4,128)S(1)}, s32[4,64]{1,0:T(4,128)}, u32[]{:S(2)}) copy-start(s32[4,64]{1,0:T(4,128)} %param.6) | copy-start | bytes 3076
  47.1 8.3 %copy-start.3 = (s32[8,128]{1,0:T(8,128)S(1)}, s32[8,128]{1,0:T(8,128)}, u32[]{:S(2)}) copy-start(s32[8,128]{1,0:T(8,128)} %param.7) | copy-start | bytes 12292
  47.8 3.8 %collective-permute-start = (f32[128,32]{1,0:T(8,128)S(1)}, f32[128,32]{1,0:T(8,128)S(1)}, u32[]{:S(2)}, u32[]{:S(2)}) collective-permute-start(f32[128,32]{1,0:T(8,128)S(1)} %get-tuple-element.179), channel_id=1, source_target_pairs={{0,1},{2,3},{4,5},{6,7},{8,9},{10,11},{12,13},{14,15},{16,17},{18,... | collective-permute-start | bytes 49160 | tf_op jit(solution)/shard_map/ppermute | solution.py:21
  50.2 3.1 %collective-permute-start.1 = (f32[128,32]{1,0:T(8,128)S(1)}, f32[128,32]{1,0:T(8,128)S(1)}, u32[]{:S(2)}, u32[]{:S(2)}) collective-permute-start(f32[128,32]{1,0:T(8,128)S(1)} %get-tuple-element.180), channel_id=1, source_target_pairs={{1,0},{3,2},{5,4},{7,6},{9,8},{11,10},{13,12},{15,14},{17,16},{19,... | collective-permute-start | bytes 49160 | tf_op jit(solution)/shard_map/ppermute | solution.py:24
  143.3 26.7 %all-to-all-start = ((bf16[1,256,4,512]{3,2,0,1:T(4,128)(2,1)}), bf16[1,256,4,512]{3,2,0,1:T(4,128)(2,1)}, u32[]{:S(2)}, u32[]{:S(2)}) async-start(bf16[1,256,4,512]{3,2,0,1:T(4,128)(2,1)} %copy.48), calls=%async_computation | async-start | bytes 2097152 | tf_op jit(solution)/shard_map/all_to_all | solution.py:134
  177.5 6.0 %copy-start = (bf16[1,2,64,8,2,2,128]{2,3,0,6,4,1,5:T(8,128)(2,1)}, bf16[1,2,64,8,2,2,128]{2,3,0,6,4,1,5:T(8,128)(2,1)S(1)}, u32[]{:S(2)}) copy-start(bf16[1,2,64,8,2,2,128]{2,3,0,6,4,1,5:T(8,128)(2,1)S(1)} %broadcast_multiply_fusion) | copy-start | bytes 3145732
  204.6 7.8 %copy-start.1 = (bf16[512,512]{1,0:T(8,128)(2,1)S(1)}, bf16[512,512]{1,0:T(8,128)(2,1)}, u32[]{:S(2)}) copy-start(bf16[512,512]{1,0:T(8,128)(2,1)} %get-tuple-element.181) | copy-start | bytes 1572868
  204.6 7.8 %copy-start.2 = (bf16[512,512]{1,0:T(8,128)(2,1)S(1)}, bf16[512,512]{1,0:T(8,128)(2,1)}, u32[]{:S(2)}) copy-start(bf16[512,512]{1,0:T(8,128)(2,1)} %get-tuple-element.182) | copy-start | bytes 1572868
Sparse Core Ops, SparseCore 0:
  55.6 82.7 all-gather.2
